TPU v7x, 256 devices: a whole 4x4x8 slice. The times are simulated.
256 devices in a mesh: seq: 32 (over z, x), head: 8 (over y, core).
Axes of the slice: x: 4, y: 4, z: 8, core: 2. Of those that a mesh axis runs over, the one named last changes fastest.
Arguments:
- queries: bfloat16 [16, 16384, 128], P(None, ('seq', 'head')), may hold values from -0.5390625 to 0.5390625
- keys: bfloat16 [16, 16384, 128], P(None, ('seq', 'head')), may hold values from -0.5390625 to 0.5390625
- values: bfloat16 [16, 16384, 128], P(None, ('seq', 'head')), may hold values from -24 to 24
- out_grad: bfloat16 [16, 16384, 128], P(None, ('seq', 'head')), may hold values from -6 to 6
- regular: float32 [16, 128], P('head'), may hold values from 0.25 to 4
Outputs:
- output: bfloat16 [16, 16384, 128], P(None, ('seq', 'head'))
- query_grad: bfloat16 [16, 16384, 128], P(None, ('seq', 'head'))
- key_grad: bfloat16 [16, 16384, 128], P(None, ('seq', 'head'))
- value_grad: bfloat16 [16, 16384, 128], P(None, ('seq', 'head'))
All inputs are finite; a program needn't handle non-finite values.
Results may differ from a plain program's by a relative error of at most 0.001.
Values may be sent and summed in bfloat16 or wider, within the bound.
No kernel may reach another device: no remote copies, remote signals or barrier semaphores. Data moves between devices by JAX's collectives and lax.ppermute only.
A program may use at most 64 MiB of HBM per device.

v0:
```python
from functools import partial

import jax
import jax.numpy as jnp
from jax import lax
from jax.sharding import PartitionSpec as P

GROUP = 128


def carried_in(part, axis, combine, identity, reverse):
    count = lax.axis_size(axis)
    place = lax.axis_index(axis)
    ahead = count - 1 - place if reverse else place
    gathered = jax.tree.map(lambda a: lax.all_gather(a, axis), part)
    state = jax.tree.map(lambda a, e: jnp.zeros_like(a) + jnp.asarray(e, a.dtype), part, identity)

    def one(lap, state):
        source = count - 1 - lap if reverse else lap
        return combine(
            state, jax.tree.map(lambda a: lax.dynamic_index_in_dim(a, source, 0, False), gathered)
        )

    return lax.fori_loop(0, ahead, one, state)


def exact_einsum(form, left, right):
    return jnp.einsum(form, left, right, precision=lax.Precision.HIGHEST)


def group_output(query_rows, key_rows, value_rows, gram_in, state_in, causal):
    eye_dim = jnp.broadcast_to(jnp.eye(gram_in.shape[-1], dtype=jnp.float32), gram_in.shape)
    low_gram = jnp.linalg.cholesky(gram_in)
    half_inv = lax.linalg.triangular_solve(low_gram, eye_dim, left_side=True, lower=True)
    inverse = lax.linalg.triangular_solve(
        low_gram, half_inv, left_side=True, lower=True, transpose_a=True
    )
    key_inv = exact_einsum("...cd,...de->...ce", key_rows, inverse)
    inner_mat = exact_einsum("...ce,...te->...ct", key_inv, key_rows)
    eye_rows = jnp.eye(causal.shape[0], dtype=jnp.float32)
    low_mix = jnp.linalg.cholesky(inner_mat + eye_rows)
    right_side = exact_einsum("...ce,...te->...ct", key_inv, query_rows)
    first_pass = (
        lax.linalg.triangular_solve(low_mix, right_side, left_side=True, lower=True) * causal
    )
    second_pass = (
        lax.linalg.triangular_solve(
            low_mix, first_pass, left_side=True, lower=True, transpose_a=True
        )
        * causal
    )
    solved = exact_einsum("...de,...te->...dt", inverse, query_rows) - exact_einsum(
        "...cd,...ct->...dt", key_inv, second_pass
    )
    scores = exact_einsum("...cd,...dt->...ct", key_rows, solved) * causal
    return exact_einsum("...ed,...dt->...te", state_in, solved) + exact_einsum(
        "...ce,...ct->...te", value_rows, scores
    )


def add_pairs(earlier, later):
    return (earlier[0] + later[0], earlier[1] + later[1])


def on_device(queries, keys, values, out_grad, regular):
    queries, keys, values, out_grad = (
        lax.all_to_all(queries, "head", split_axis=0, concat_axis=1, tiled=True),
        lax.all_to_all(keys, "head", split_axis=0, concat_axis=1, tiled=True),
        lax.all_to_all(values, "head", split_axis=0, concat_axis=1, tiled=True),
        lax.all_to_all(out_grad, "head", split_axis=0, concat_axis=1, tiled=True),
    )
    head_count, token_count, feature = keys.shape
    group_len = GROUP
    block_count = token_count // group_len
    block_shape = (head_count, block_count, group_len, feature)
    key_blocks = keys.reshape(block_shape)
    value_blocks = values.reshape(block_shape)
    grams = jnp.einsum(
        "hncd,hnce->hnde", key_blocks, key_blocks, preferred_element_type=jnp.float32
    )
    states = jnp.einsum(
        "hnce,hncd->hned", value_blocks, key_blocks, preferred_element_type=jnp.float32
    )
    zero_block = jnp.zeros_like(grams[:, :1])
    gram_local = jnp.concatenate([zero_block, jnp.cumsum(grams, axis=1)[:, :-1]], axis=1)
    state_local = jnp.concatenate([zero_block, jnp.cumsum(states, axis=1)[:, :-1]], axis=1)
    total_gram = jnp.sum(grams, axis=1)
    total_state = jnp.sum(states, axis=1)
    zero_total = jnp.zeros_like(total_gram)
    lower_gram, lower_state = carried_in(
        (total_gram, total_state), "seq", add_pairs, (zero_total, zero_total), False
    )
    base = regular[:, :, None] * jnp.eye(feature, dtype=jnp.float32)
    gram_in = base[:, None] + (lower_gram[:, None] + gram_local)
    state_in = lower_state[:, None] + state_local
    positions = jnp.arange(group_len)
    causal = (positions[:, None] <= positions[None, :]).astype(jnp.float32)
    query_full = queries.reshape(block_shape).astype(jnp.float32)
    key_full = key_blocks.astype(jnp.float32)
    value_full = value_blocks.astype(jnp.float32)
    grad_full = out_grad.reshape(block_shape).astype(jnp.float32)
    result, pull = jax.vjp(
        partial(group_output, causal=causal), query_full, key_full, value_full, gram_in, state_in
    )
    dq_part, dk_part, dv_part, dgram_part, dstate_part = pull(grad_full)
    gram_incl = jnp.flip(jnp.cumsum(jnp.flip(dgram_part, 1), axis=1), 1)
    state_incl = jnp.flip(jnp.cumsum(jnp.flip(dstate_part, 1), axis=1), 1)
    gram_after = jnp.concatenate([gram_incl[:, 1:], zero_block], axis=1)
    state_after = jnp.concatenate([state_incl[:, 1:], zero_block], axis=1)
    grad_gram_total = gram_incl[:, 0]
    grad_state_total = state_incl[:, 0]
    upper_gram, upper_state = carried_in(
        (grad_gram_total, grad_state_total), "seq", add_pairs, (zero_total, zero_total), True
    )
    gram_later = upper_gram[:, None] + gram_after
    state_later = upper_state[:, None] + state_after
    sym_later = gram_later + jnp.swapaxes(gram_later, -1, -2)
    dk_total = (
        dk_part
        + exact_einsum("hnde,hnce->hncd", sym_later, key_full)
        + exact_einsum("hned,hnce->hncd", state_later, value_full)
    )
    dv_total = dv_part + exact_einsum("hned,hncd->hnce", state_later, key_full)
    flat_shape = (head_count, token_count, feature)
    output = result.reshape(flat_shape).astype(jnp.bfloat16)
    query_grad = dq_part.reshape(flat_shape).astype(jnp.bfloat16)
    key_grad = dk_total.reshape(flat_shape).astype(jnp.bfloat16)
    value_grad = dv_total.reshape(flat_shape).astype(jnp.bfloat16)
    return (
        lax.all_to_all(output, "head", split_axis=1, concat_axis=0, tiled=True),
        lax.all_to_all(query_grad, "head", split_axis=1, concat_axis=0, tiled=True),
        lax.all_to_all(key_grad, "head", split_axis=1, concat_axis=0, tiled=True),
        lax.all_to_all(value_grad, "head", split_axis=1, concat_axis=0, tiled=True),
    )


def solution(mesh):
    placed = (
        P(None, ("seq", "head"), None),
        P(None, ("seq", "head"), None),
        P(None, ("seq", "head"), None),
        P(None, ("seq", "head"), None),
        P("head", None),
    )
    return jax.shard_map(
        on_device,
        mesh=mesh,
        in_specs=placed,
        out_specs=(
            P(None, ("seq", "head"), None),
            P(None, ("seq", "head"), None),
            P(None, ("seq", "head"), None),
            P(None, ("seq", "head"), None),
        ),
        check_vma=False,
    )
```

profile of v0, /device:TPU:1, one launch (start us, length us, event | category | flops | bytes accessed | tf_op | source)
XLA Modules:
  0.0 1041.7 jit_solution(14517218476108788780)
XLA Ops:
  7.2 13.0 %all_to_all.132 = bf16[16,64,128]{2,1,0:T(8,128)(2,1)S(1)} all-to-all(bf16[16,64,128]{2,1,0:T(8,128)(2,1)} %param.22), channel_id=1, replica_groups=mesh['seq'=32,'head'=8] {'head'}, dimensions={0} | all-to-all | bytes 524288 | tf_op jit(solution)/shard_map/all_to_all | solution.py:68
  20.2 4.4 all-to-all-start.1
  24.5 6.5 all-to-all-done.1
  33.0 4.4 all-to-all-start.2
  38.8 5.1 all-to-all-done.2
  43.9 4.4 all-to-all-start.4
  48.3 6.4 all-to-all-done.4
  56.8 54.4 %all-gather.11.cloned.1.call-done = f32[64,128,128]{2,1,0:T(8,128)} async-done(((f32[2,128,128]{2,1,0:T(8,128)}), f32[64,128,128]{2,1,0:T(8,128)}) %all-gather.11.cloned.1.call-update) | async-done | bytes 4194320 | tf_op jit(solution)/shard_map/all_gather | solution.py:15
  111.2 81.7 %all-gather.9.cloned.1.call-done = f32[64,128,128]{2,1,0:T(8,128)} async-done(((f32[2,128,128]{2,1,0:T(8,128)}), f32[64,128,128]{2,1,0:T(8,128)}) %all-gather.9.cloned.1.call-update) | async-done | bytes 4194320 | tf_op jit(solution)/shard_map/all_gather | solution.py:15
  193.4 93.8 %custom-call.27 = f32[2,4,128,128]{3,2,1,0:T(8,128)S(1)} custom-call(f32[2,4,128,128]{3,2,1,0:T(8,128)S(1)} %fusion.55), custom_call_target="Cholesky" | custom-call | tf_op jit(solution)/shard_map/jvp(jit(cholesky))/cholesky | solution.py:33
  288.4 78.8 %custom-call.29 = f32[2,4,1,128,128]{3,4,2,1,0:T(8,128)S(1)} custom-call(f32[2,4,1,128,128]{4,3,2,1,0:T(8,128)S(1)} %get-tuple-element.201), custom_call_target="InvertDiagBlocksLowerTriangular" | custom-call | tf_op jit(solution)/shard_map/jvp()/triangular_solve/custom-call.0 | solution.py:35
  381.1 94.6 %custom-call.30 = f32[2,4,128,128]{3,2,1,0:T(8,128)S(1)} custom-call(f32[2,4,128,128]{3,2,1,0:T(8,128)} %fusion.46), custom_call_target="Cholesky" | custom-call | tf_op jit(solution)/shard_map/jvp(jit(cholesky))/cholesky | solution.py:41
  477.6 79.0 %custom-call.32 = f32[2,4,1,128,128]{3,4,2,1,0:T(8,128)S(1)} custom-call(f32[2,4,1,128,128]{4,3,2,1,0:T(8,128)S(1)} %get-tuple-element.203), custom_call_target="InvertDiagBlocksLowerTriangular" | custom-call | tf_op jit(solution)/shard_map/jvp()/triangular_solve/custom-call.0 | solution.py:47
  565.9 80.2 %custom-call.37 = f32[2,4,1,128,128]{3,4,2,1,0:T(8,128)} custom-call(f32[2,4,1,128,128]{4,3,2,1,0:T(8,128)} %get-tuple-element.202), custom_call_target="InvertDiagBlocksLowerTriangular" | custom-call | tf_op jit(solution)/shard_map/transpose(jvp(jit(cholesky)))/triangular_solve/custom-call.0 | solution.py:41
  667.0 80.2 %custom-call.42 = f32[2,4,1,128,128]{3,4,2,1,0:T(8,128)} custom-call(f32[2,4,1,128,128]{4,3,2,1,0:T(8,128)} %get-tuple-element.200), custom_call_target="InvertDiagBlocksLowerTriangular" | custom-call | tf_op jit(solution)/shard_map/transpose(jvp(jit(cholesky)))/triangular_solve/custom-call.0 | solution.py:33
  782.7 8.8 all-to-all-start.5
  807.3 70.8 %all-gather.13.cloned.1.call-done = f32[64,1,128,128]{3,2,1,0:T(8,128)} async-done(((f32[2,1,128,128]{3,2,1,0:T(8,128)}), f32[64,1,128,128]{3,2,1,0:T(8,128)}) %all-gather.13.cloned.1.call-update) | async-done | bytes 4194320 | tf_op jit(solution)/shard_map/all_gather | solution.py:15
  878.1 81.0 %all-gather.15.cloned.1.call-done = f32[64,1,128,128]{3,2,1,0:T(8,128)} async-done(((f32[2,1,128,128]{3,2,1,0:T(8,128)}), f32[64,1,128,128]{3,2,1,0:T(8,128)}) %all-gather.15.cloned.1.call-update) | async-done | bytes 4194320 | tf_op jit(solution)/shard_map/all_gather | solution.py:15
  959.1 33.0 %while.27 = (s32[]{:T(128)}, f32[2,128,128]{2,1,0:T(8,128)S(1)}, f32[2,128,128]{2,1,0:T(8,128)S(1)}, s32[]{:T(128)}, f32[32,2,128,128]{3,2,1,0:T(8,128)}, /*inde...) while((s32[]{:T(128)}, f32[2,128,128]{2,1,0:T(8,128)S(1)}, ...), condition=%wide.region_11.16_spmd, body=%wide.region_10.15_spmd.sunk | while | flops 65542 | bytes 786591 | solution.py:24
  997.3 8.5 all-to-all-start.3
  1006.4 5.8 all-to-all-done.3
  1012.2 4.4 all-to-all-start.7
  1023.1 4.4 all-to-all-start.6
  1030.7 3.3 all-to-all-done.6
  (237 shorter events, 152.2 us)
Async XLA Ops:
  7.2 41.1 %copy-start.41 = (f32[2,128]{1,0:T(2,128)S(1)}, f32[2,128]{1,0:T(2,128)}, u32[]{:S(2)}) copy-start(f32[2,128]{1,0:T(2,128)} %param.25) | copy-start | bytes 3076
  20.2 10.9 %all-to-all-start.1 = ((bf16[16,64,128]{2,1,0:T(8,128)(2,1)}), bf16[16,64,128]{2,1,0:T(8,128)(2,1)S(1)}, u32[]{:S(2)}, u32[]{:S(2)}) async-start(bf16[16,64,128]{2,1,0:T(8,128)(2,1)} %param.23), calls=%async_computation.1 | async-start | bytes 524288 | tf_op jit(solution)/shard_map/all_to_all | solution.py:69
  24.5 86.7 %all-gather.11.cloned.1.call-start = ((), (), s32[]{:S(2)}) async-start(), calls=%async_computation.9 | async-start | bytes 4325376 | tf_op jit(solution)/shard_map/all_gather | solution.py:15
  32.0 160.9 %all-gather.9.cloned.1.call-start = ((), (), s32[]{:S(2)}) async-start(), calls=%async_computation.8 | async-start | bytes 4325376 | tf_op jit(solution)/shard_map/all_gather | solution.py:15
  33.0 10.9 %all-to-all-start.2 = ((bf16[16,64,128]{2,1,0:T(8,128)(2,1)}), bf16[16,64,128]{2,1,0:T(8,128)(2,1)S(1)}, u32[]{:S(2)}, u32[]{:S(2)}) async-start(bf16[16,64,128]{2,1,0:T(8,128)(2,1)} %param.21), calls=%async_computation.2 | async-start | bytes 524288 | tf_op jit(solution)/shard_map/all_to_all | solution.py:67
  37.4 249.8 %copy-start.34 = (pred[128,128]{1,0:T(8,128)(4,1)}, pred[128,128]{1,0:T(8,128)(4,1)S(1)}, u32[]{:S(2)}) copy-start(pred[128,128]{1,0:T(8,128)(4,1)S(1)} %iota_compare_fusion.3) | copy-start | bytes 49156
  37.4 336.1 %copy-start.17 = (f32[128,128]{1,0:T(8,128)}, f32[128,128]{1,0:T(8,128)S(1)}, u32[]{:S(2)}) copy-start(f32[128,128]{1,0:T(8,128)S(1)} %fusion.80) | copy-start | bytes 196612
  43.9 10.9 %all-to-all-start.4 = ((bf16[16,64,128]{2,1,0:T(8,128)(2,1)}), bf16[16,64,128]{2,1,0:T(8,128)(2,1)S(1)}, u32[]{:S(2)}, u32[]{:S(2)}) async-start(bf16[16,64,128]{2,1,0:T(8,128)(2,1)} %param.24), calls=%async_computation.4 | async-start | bytes 524288 | tf_op jit(solution)/shard_map/all_to_all | solution.py:70
  48.3 829.8 %all-gather.13.cloned.1.call-start = ((), (), s32[]{:S(2)}) async-start(), calls=%async_computation.10 | async-start | bytes 4325376 | tf_op jit(solution)/shard_map/all_gather | solution.py:15
  48.3 328.3 %copy-start.5 = (bf16[8,2,64,128]{3,2,0,1:T(8,128)(2,1)}, bf16[8,2,64,128]{3,2,0,1:T(8,128)(2,1)S(1)}, u32[]{:S(2)}) copy-start(bf16[8,2,64,128]{3,2,0,1:T(8,128)(2,1)S(1)} %copy.280) | copy-start | bytes 786436
  54.8 316.7 %copy-start.3 = (bf16[8,2,64,128]{3,2,0,1:T(8,128)(2,1)}, bf16[8,2,64,128]{3,2,0,1:T(8,128)(2,1)S(1)}, u32[]{:S(2)}) copy-start(bf16[8,2,64,128]{3,2,0,1:T(8,128)(2,1)S(1)} %copy.295) | copy-start | bytes 786436
  56.8 324.4 %copy-start.9 = (f32[2,4,128,128]{3,2,1,0:T(8,128)}, f32[2,4,128,128]{3,2,1,0:T(8,128)S(1)}, u32[]{:S(2)}) copy-start(f32[2,4,128,128]{3,2,1,0:T(8,128)S(1)} %convolution_multiply_fusion.2) | copy-start | bytes 1572868
  193.0 174.3 %copy-start.33 = (f32[128,128]{0,1:T(8,128)S(1)}, f32[128,128]{0,1:T(8,128)}, u32[]{:S(2)}) copy-start(f32[128,128]{0,1:T(8,128)} %copy-done.32) | copy-start | bytes 196612
  287.2 80.0 %copy-start.27 = (f32[2,4,128,128]{3,2,1,0:T(8,128)}, f32[2,4,128,128]{3,2,1,0:T(8,128)S(1)}, u32[]{:S(2)}) copy-start(f32[2,4,128,128]{3,2,1,0:T(8,128)S(1)} %custom-call.27) | copy-start | bytes 1572868
  560.2 91.6 %copy-start = (f32[2,4,128,128]{3,2,1,0:T(8,128)}, f32[2,4,128,128]{3,2,1,0:T(8,128)S(1)}, u32[]{:S(2)}) copy-start(f32[2,4,128,128]{3,2,1,0:T(8,128)S(1)} %fusion.44) | copy-start | bytes 1572868
  662.7 84.5 %copy-start.11 = (f32[2,4,128,128]{3,2,1,0:T(8,128)S(1)}, f32[2,4,128,128]{3,2,1,0:T(8,128)}, u32[]{:S(2)}) copy-start(f32[2,4,128,128]{3,2,1,0:T(8,128)} %copy-done.10) | copy-start | bytes 1572868
  767.8 191.2 %all-gather.15.cloned.1.call-start = ((), (), s32[]{:S(2)}) async-start(), calls=%async_computation.11 | async-start | bytes 4325376 | tf_op jit(solution)/shard_map/all_gather | solution.py:15
  782.7 214.6 %all-to-all-start.5 = ((bf16[2,512,128]{2,0,1:T(2,128)(2,1)}), bf16[2,512,128]{2,0,1:T(2,128)(2,1)}, u32[]{:S(2)}, u32[]{:S(2)}) async-start(bf16[2,512,128]{2,0,1:T(2,128)(2,1)} %copy.305), calls=%async_computation.5 | async-start | bytes 524288 | tf_op jit(solution)/shard_map/all_to_all | solution.py:131
  804.4 187.9 %copy-start.20 = (f32[2,3,128,128]{2,3,1,0:T(8,128)S(1)}, f32[2,3,128,128]{2,3,1,0:T(8,128)}, u32[]{:S(2)}) copy-start(f32[2,3,128,128]{2,3,1,0:T(8,128)} %slice.45) | copy-start | bytes 1179652
  804.4 189.3 %copy-start.19 = (f32[2,3,128,128]{3,2,1,0:T(8,128)S(1)}, f32[2,3,128,128]{3,2,1,0:T(8,128)}, u32[]{:S(2)}) copy-start(f32[2,3,128,128]{3,2,1,0:T(8,128)} %slice.43) | copy-start | bytes 1179652
  807.3 184.9 %copy-start.23 = (f32[2,4,128,128]{3,2,1,0:T(8,128)S(1)}, f32[2,4,128,128]{3,2,1,0:T(8,128)}, u32[]{:S(2)}) copy-start(f32[2,4,128,128]{3,2,1,0:T(8,128)} %fusion.107) | copy-start | bytes 1572868
  997.3 15.0 %all-to-all-start.3 = ((bf16[2,512,128]{2,0,1:T(2,128)(2,1)}), bf16[2,512,128]{2,0,1:T(2,128)(2,1)S(1)}, u32[]{:S(2)}, u32[]{:S(2)}) async-start(bf16[2,512,128]{2,0,1:T(2,128)(2,1)} %copy.293), calls=%async_computation.3 | async-start | bytes 524288 | tf_op jit(solution)/shard_map/all_to_all | solution.py:130
  1012.2 10.9 %all-to-all-start.7 = ((bf16[2,512,128]{2,0,1:T(2,128)(2,1)}), bf16[2,512,128]{2,0,1:T(2,128)(2,1)S(1)}, u32[]{:S(2)}, u32[]{:S(2)}) async-start(bf16[2,512,128]{2,0,1:T(2,128)(2,1)} %copy.340), calls=%async_computation.7 | async-start | bytes 524288 | tf_op jit(solution)/shard_map/all_to_all | solution.py:133
  1023.1 10.9 %all-to-all-start.6 = ((bf16[2,512,128]{2,0,1:T(2,128)(2,1)}), bf16[2,512,128]{2,0,1:T(2,128)(2,1)S(1)}, u32[]{:S(2)}, u32[]{:S(2)}) async-start(bf16[2,512,128]{2,0,1:T(2,128)(2,1)} %copy.337), calls=%async_computation.6 | async-start | bytes 524288 | tf_op jit(solution)/shard_map/all_to_all | solution.py:132
  (29 other events, 224.4 us)
Sparse Core Ops, SparseCore 0:
  32.1 79.0 all-gather.10
  114.4 78.5 all-gather.8
  768.0 110.0 all-gather.12
  880.5 78.5 all-gather.14
where the time goes:
time: 1050 us; the launch traced here: 1040 us
  other arithmetic  555 us (53%)
  waiting for transfers between devices  318 us (30%)
  matrix products  68.6 us (7%)
  starting transfers between devices  39.2 us (4%)
  local copies, waits for them, and re-layouts  32.4 us (3%)
  between operations  15.1 us (1%)
  blocking collectives  13 us (1%)
    all_gather x4, waiting for transfers between devices, carried_in(): gathered = jax.tree.map(lambda a: lax.all_gather(a, axis), part)  288 us
    another operation x5, other arithmetic, group_output(): low_mix = jnp.linalg.cholesky(inner_mat + eye_rows)  177 us
    another operation x6, other arithmetic, group_output(): low_gram = jnp.linalg.cholesky(gram_in)  175 us
    another operation x1, other arithmetic, group_output(): lax.linalg.triangular_solve(low_mix, first_pass, left_side=True, lower=Tr...  79 us
    another operation x1, other arithmetic, group_output(): lax.linalg.triangular_solve(low_gram, half_inv, left_side=True, lower=Tru...  78.8 us
    dot_general x27, matrix products, exact_einsum(): return jnp.einsum(form, left, right, precision=lax.Precision.HIGHEST)  37 us
    add x31, other arithmetic, add_pairs(): return (earlier[0] + later[0], earlier[1] + later[1])  32.3 us
  transfers between devices with their start and end apart: 11, of which 10 were waited for; matrix products, arithmetic and copies ran while one was open for 7% of the time, Pallas kernels for 0%

commit v1 on v0

v1 whole, which is shorter than its diff:
```python
import jax
import jax.numpy as jnp
from jax import lax
from jax.experimental import pallas as pl
from jax.experimental.pallas import tpu as pltpu
from jax.sharding import PartitionSpec as P

F32 = jnp.float32
BF16 = jnp.bfloat16
BLOCK = 128
DIM = 128
TILE = 8
PARAMS = pltpu.CompilerParams(vmem_limit_bytes=56 * 1024 * 1024)


def halves(x):
    high = x.astype(BF16)
    return high, (x - high.astype(F32)).astype(BF16)


def thirds(x):
    high = x.astype(BF16)
    rest = x - high.astype(F32)
    mid = rest.astype(BF16)
    return high, mid, (rest - mid.astype(F32)).astype(BF16)


def contract(pairs, left_dim, right_dim):
    left = [a for a, _ in pairs]
    right = [b for _, b in pairs]
    left = left[0] if len(left) == 1 else jnp.concatenate(left, axis=left_dim)
    right = right[0] if len(right) == 1 else jnp.concatenate(right, axis=right_dim)
    return lax.dot_general(
        left, right, (((left_dim,), (right_dim,)), ((), ())), preferred_element_type=F32
    )


def cross(left, right):
    return [(left[0], right[0]), (left[0], right[1]), (left[1], right[0])]


def owned_rows(ref, block, which):
    first = 2 * block
    second = first + 1
    return jnp.concatenate(
        [
            ref[2 * (first % 8) + first // 8, which],
            ref[2 * (second % 8) + second // 8, which],
        ],
        axis=0,
    )


def put_rows(ref, block, which, rows):
    half = BLOCK // 2
    first = 2 * block
    second = first + 1
    ref[2 * (first % 8) + first // 8, which] = rows[:half]
    ref[2 * (second % 8) + second // 8, which] = rows[half:]


def stacked(ref, which):
    return jnp.concatenate([ref[i, which] for i in range(ref.shape[0])], axis=0)


def put_stacked(ref, which, rows):
    for i in range(ref.shape[0]):
        ref[i, which] = rows[TILE * i : TILE * (i + 1)]


def factor(mats, count):
    lane = lax.broadcasted_iota(jnp.int32, (TILE, DIM), 1)
    row = lax.broadcasted_iota(jnp.int32, (TILE, DIM), 0)

    def panel(step, start):
        base = pl.multiple_of(step * TILE, TILE)
        rel = lane - base
        inside = (rel >= 0) & (rel < TILE)
        after = rel >= TILE
        unit = jnp.where(rel == row, 1.0, 0.0).astype(F32)
        rows = [mats[n, pl.ds(base, TILE), :] for n in range(count)]
        cols = [
            [jnp.take_along_axis(rows[n], jnp.full((TILE, DIM), 0, jnp.int32) + (base + j), axis=1) for j in range(TILE)]
            for n in range(count)
        ]
        rows = [jnp.where(inside, unit, r) for r in rows]
        for k in range(TILE):
            for n in range(count):
                col = cols[n]
                scale = lax.rsqrt(jnp.broadcast_to(col[k][k : k + 1], (TILE, DIM)))
                pivot = jnp.broadcast_to(rows[n][k : k + 1], (TILE, DIM)) * scale
                mult = jnp.where(row > k, col[k] * scale, 0.0)
                rows[n] = jnp.where(row == k, pivot, rows[n] - mult * pivot)
                for j in range(k + 1, TILE):
                    col[j] = col[j] - mult * (jnp.broadcast_to(col[j][k : k + 1], (TILE, DIM)) * scale)
        for n in range(count):
            high, mid, low = thirds(rows[n])
            none = jnp.zeros_like(rows[n])
            lh = jnp.where(after, high.astype(F32), none)
            lm = jnp.where(after, mid.astype(F32), none)
            ll = jnp.where(after, low.astype(F32), none)
            rh, rm, rl = high.astype(F32), mid.astype(F32), low.astype(F32)
            left = jnp.concatenate([lh, lh, lm, lm, lh, ll], axis=0).astype(BF16)
            right = jnp.concatenate([rh, rm, rh, rm, rl, rh], axis=0).astype(BF16)
            left = left[:, start:]
            change = lax.dot_general(
                left, right, (((0,), (0,)), ((), ())), preferred_element_type=F32
            )
            old = mats[n, start:, :]
            keep = jnp.concatenate([inside] * ((DIM - start) // TILE), axis=0)
            mats[n, start:, :] = jnp.where(keep, 0.0, old) - change
            mats[n, pl.ds(base, TILE), :] = rows[n]

    def run(step, carry):
        panel(step, 0)
        return carry

    lax.fori_loop(0, DIM // TILE, run, 0)


def totals_kernel(own_ref, total_ref):
    gram = jnp.zeros((DIM, DIM), F32)
    state = jnp.zeros((DIM, DIM), F32)
    for n in range(8):
        k = owned_rows(own_ref, n, 1)
        v = owned_rows(own_ref, n, 2)
        gram = gram + contract([(k, k)], 0, 0)
        state = state + contract([(v, k)], 0, 0)
    put_stacked(total_ref, 0, gram)
    put_stacked(total_ref, 1, state)


def scan_kernel(part_ref, out_ref, *, reverse):
    count = part_ref.shape[0]
    order = range(count - 1, -1, -1) if reverse else range(count)
    total = jnp.zeros(part_ref.shape[1:], F32)
    for i in order:
        out_ref[i] = total
        total = total + part_ref[i]


def main_kernel(
    own_ref, before_ref, reg_ref, early_ref, dk_ref, dv_ref, dgram_ref, dstate_ref, total_ref,
    mats, state_in, inverse, key_inv,
):
    wide = lax.broadcasted_iota(jnp.int32, (DIM, DIM), 1)
    tall = lax.broadcasted_iota(jnp.int32, (DIM, DIM), 0)
    lower = tall >= wide
    causal2 = jnp.concatenate([lower, lower], axis=0)
    gram = jnp.where(tall == wide, jnp.broadcast_to(reg_ref[...], (DIM, DIM)), 0.0) + stacked(before_ref, 0)
    state = stacked(before_ref, 1)
    for n in range(8):
        mats[n] = gram
        state_in[n] = state
        if n < 7:
            k = owned_rows(own_ref, n, 1)
            v = owned_rows(own_ref, n, 2)
            gram = gram + contract([(k, k)], 0, 0)
            state = state + contract([(v, k)], 0, 0)
    factor(mats, 8)

    def middle(n):
        low = halves(jnp.where(lower, mats[n], 0.0))
        inv = contract(cross(low, low), 0, 0)
        inv = halves(inv)
        inverse[n, 0] = inv[0]
        inverse[n, 1] = inv[1]
        k = owned_rows(own_ref, n, 1)
        ki = halves(contract([(k, inv[0]), (k, inv[1])], 1, 0))
        key_inv[n, 0] = ki[0]
        key_inv[n, 1] = ki[1]
        mats[n] = contract([(ki[0], k), (ki[1], k)], 1, 1) + jnp.where(tall == wide, 1.0, 0.0)

    def middle_two(i, carry):
        middle(2 * i)
        middle(2 * i + 1)
        return carry

    lax.fori_loop(0, 4, middle_two, 0)
    factor(mats, 8)

    def solve(n):
        q = owned_rows(own_ref, n, 0)
        k = owned_rows(own_ref, n, 1)
        v = owned_rows(own_ref, n, 2)
        g = owned_rows(own_ref, n, 3)
        st = halves(state_in[n])
        inv = (inverse[n, 0], inverse[n, 1])
        ki = (key_inv[n, 0], key_inv[n, 1])
        low = halves(jnp.where(lower, mats[n], 0.0))
        ds = jnp.where(lower, contract([(g, v)], 1, 1), 0.0)
        dsh = halves(ds)
        du = contract([(g, st[0]), (g, st[1]), (dsh[0], k), (dsh[1], k)], 1, 0)
        duh = halves(du)
        rhs = (
            jnp.concatenate([q, duh[0]], axis=0),
            jnp.concatenate([jnp.zeros_like(q), duh[1]], axis=0),
        )
        r = halves(contract(cross(rhs, ki), 1, 1))
        y = halves(jnp.where(causal2, contract(cross(r, low), 1, 1), 0.0))
        x = halves(-contract(cross(y, low), 1, 0))
        uz = contract(cross(rhs, inv) + cross(x, ki), 1, 0)
        uzh = halves(uz)
        ss = jnp.where(causal2, contract([(uzh[0], k), (uzh[1], k)], 1, 1), 0.0)
        u = (uzh[0][:BLOCK], uzh[1][:BLOCK])
        z = (uzh[0][BLOCK:], uzh[1][BLOCK:])
        s = halves(ss[:BLOCK])
        out = contract(cross(u, st), 1, 1) + contract([(s[0], v), (s[1], v)], 1, 0)
        put_rows(early_ref, n, 0, out.astype(BF16))
        put_rows(early_ref, n, 1, uz[BLOCK:].astype(BF16))
        e = halves(ds - ss[BLOCK:])
        neg = (-s[0], -s[1])
        dk_ref[n] = contract(cross(e, u) + cross(neg, z), 0, 0)
        dv_ref[n] = contract([(s[0], g), (s[1], g)], 0, 0)
        dstate = contract([(g, u[0]), (g, u[1])], 0, 0)
        dgram = -contract(cross(z, u), 0, 0)
        dgram_ref[n] = dgram
        dstate_ref[n] = dstate
        return dgram, dstate

    def solve_two(i, carry):
        a = solve(2 * i)
        b = solve(2 * i + 1)
        return carry[0] + (a[0] + b[0]), carry[1] + (a[1] + b[1])

    zero = jnp.zeros((DIM, DIM), F32)
    sums = lax.fori_loop(0, 4, solve_two, (zero, zero))
    put_stacked(total_ref, 0, sums[0])
    put_stacked(total_ref, 1, sums[1])


def final_kernel(own_ref, after_ref, dk_ref, dv_ref, dgram_ref, dstate_ref, late_ref):
    gram = stacked(after_ref, 0)
    state = stacked(after_ref, 1)
    for n in range(7, -1, -1):
        k = owned_rows(own_ref, n, 1)
        v = owned_rows(own_ref, n, 2)
        sym = halves(gram + gram.T)
        st = halves(state)
        dk = dk_ref[n] + contract([(k, sym[0]), (k, sym[1]), (v, st[0]), (v, st[1])], 1, 0)
        dv = dv_ref[n] + contract([(k, st[0]), (k, st[1])], 1, 1)
        put_rows(late_ref, n, 0, dk.astype(BF16))
        put_rows(late_ref, n, 1, dv.astype(BF16))
        if n > 0:
            gram = gram + dgram_ref[n]
            state = state + dstate_ref[n]


def local_totals(own):
    return pl.pallas_call(
        totals_kernel,
        out_shape=jax.ShapeDtypeStruct((16, 2, TILE, DIM), F32),
        compiler_params=PARAMS,
        name="totals",
    )(own)


def scan_parts(parts, reverse):
    def body(part_ref, out_ref):
        scan_kernel(part_ref, out_ref, reverse=reverse)

    return pl.pallas_call(
        body, out_shape=jax.ShapeDtypeStruct(parts.shape, F32), name="scan_rev" if reverse else "scan_fwd"
    )(parts)


def main_part(own, before, reg):
    full = jax.ShapeDtypeStruct((8, DIM, DIM), F32)
    return pl.pallas_call(
        main_kernel,
        out_shape=(
            jax.ShapeDtypeStruct((16, 2, BLOCK // 2, DIM), BF16),
            full, full, full, full,
            jax.ShapeDtypeStruct((16, 2, TILE, DIM), F32),
        ),
        scratch_shapes=[
            pltpu.VMEM((8, DIM, DIM), F32),
            pltpu.VMEM((8, DIM, DIM), F32),
            pltpu.VMEM((8, 2, DIM, DIM), BF16),
            pltpu.VMEM((8, 2, DIM, DIM), BF16),
        ],
        compiler_params=PARAMS,
        name="main",
    )(own, before, reg)


def final_part(own, after, dk, dv, dgram, dstate):
    return pl.pallas_call(
        final_kernel,
        out_shape=jax.ShapeDtypeStruct((16, 2, BLOCK // 2, DIM), BF16),
        compiler_params=PARAMS,
        name="final",
    )(own, after, dk, dv, dgram, dstate)


AXES = ("seq", "head")
TOKEN_GROUPS = [[(2 * m + h % 2) * 8 + h // 2 for h in range(16)] for m in range(16)]
SCAN_GROUPS = [[16 * m + r for m in range(16)] for r in range(16)]


def swap(array, groups):
    return lax.all_to_all(array, AXES, 0, 0, axis_index_groups=groups)


def carried(total, reverse):
    return swap(scan_parts(swap(total, SCAN_GROUPS), reverse), SCAN_GROUPS)


def on_device(queries, keys, values, out_grad, regular):
    own = swap(jnp.stack([queries, keys, values, out_grad], axis=1), TOKEN_GROUPS)
    reg = lax.dynamic_slice_in_dim(regular, lax.axis_index("seq") % 2, 1, 0)
    before = carried(local_totals(own), False)
    early, dk, dv, dgram, dstate, total = main_part(own, before, reg)
    after = carried(total, True)
    late = final_part(own, after, dk, dv, dgram, dstate)
    back = swap(jnp.concatenate([early, late], axis=1), TOKEN_GROUPS)
    return back[:, 0], back[:, 1], back[:, 2], back[:, 3]


def solution(mesh):
    placed = P(None, ("seq", "head"), None)
    return jax.shard_map(
        on_device,
        mesh=mesh,
        in_specs=(placed, placed, placed, placed, P("head", None)),
        out_specs=(placed, placed, placed, placed),
        check_vma=False,
    )
```

time: 1050 us -> 155 us (0.15)
  other arithmetic: 555 us -> 2.46 us
  waiting for transfers between devices: 318 us -> 9.59 us
  blocking collectives: 13 us -> 94.8 us
  matrix products: 68.6 us -> 0 us
  Pallas kernels: 0 us -> 41.2 us
  starting transfers between devices: 39.2 us -> 3.51 us
  local copies, waits for them, and re-layouts: 32.4 us -> 2.17 us
  between operations: 15.1 us -> 0.69 us
    another operation x17 -> x1, other arithmetic: 513 us -> 1.32 us  [on_device(): jnp.stack([queries, keys, values, out_grad], axis=1)]
    all_gather x4 -> x0, waiting for transfers between devices: 288 us -> none  [carried_in(): gathered = jax.tree.map(lambda a: lax.all_gather(a, axis), part)]
    all_to_all x1 -> x5, blocking collectives: 13 us -> 94.8 us  [swap(): return lax.all_to_all(array, AXES, 0, 0, axis_index_groups=groups)]
    dot_general x35 -> x0, matrix products: 49.7 us -> none  [the longest x27 37 us: exact_einsum(): return jnp.einsum(form, left, right, precision=lax.Precision.HIGHEST)]
    pallas_call x0 -> x5, Pallas kernels: none -> 41.2 us  [the longest x1 32.4 us: main_part(): pl.pallas_call(main_kernel, out_shape=(jax.ShapeDtypeStruct((16, 2, BLOCK...]
    all_to_all x7 -> x1, starting transfers between devices: 39.1 us -> 3.51 us  [swap(): return lax.all_to_all(array, AXES, 0, 0, axis_index_groups=groups)]
    add x34 -> x0, other arithmetic: 33.2 us -> none  [the longest x31 32.3 us: add_pairs(): return (earlier[0] + later[0], earlier[1] + later[1])]
    all_to_all x7 -> x1, waiting for transfers between devices: 30.1 us -> 9.59 us  [swap(): return lax.all_to_all(array, AXES, 0, 0, axis_index_groups=groups)]
  transfers between devices with their start and end apart: 11 -> 1, of which waited for: 10 -> 1; matrix products, arithmetic and copies ran while one was open for 7% -> 0% of each run, Pallas kernels for 0% -> 0%
where the time goes in v1:
time: 155 us; the launch traced here: 154 us
  blocking collectives  94.8 us (61%)
  Pallas kernels  41.2 us (27%)
  waiting for transfers between devices  9.59 us (6%)
  starting transfers between devices  3.51 us (2%)
  other arithmetic  2.46 us (2%)
  local copies, waits for them, and re-layouts  2.17 us (1%)
    all_to_all x5, blocking collectives, swap(): return lax.all_to_all(array, AXES, 0, 0, axis_index_groups=groups)  94.8 us
    pallas_call x1, Pallas kernels, main_part(): pl.pallas_call(main_kernel, out_shape=(jax.ShapeDtypeStruct((16, 2, BLOCK...  32.4 us
    all_to_all x1, waiting for transfers between devices, swap(): return lax.all_to_all(array, AXES, 0, 0, axis_index_groups=groups)  9.59 us
    all_to_all x1, starting transfers between devices, swap(): return lax.all_to_all(array, AXES, 0, 0, axis_index_groups=groups)  3.51 us
    pallas_call x1, Pallas kernels, final_part(): pl.pallas_call(final_kernel, out_shape=jax.ShapeDtypeStruct((16, 2, BLOCK...  3.41 us
    pallas_call x2, Pallas kernels, scan_parts(): pl.pallas_call(body, out_shape=jax.ShapeDtypeStruct(parts.shape, F32), na...  3.15 us
  transfers between devices with their start and end apart: 1, of which 1 were waited for; matrix products, arithmetic and copies ran while one was open for 0% of the time, Pallas kernels for 0%

profile of v1, /device:TPU:1, one launch (start us, length us, event | category | flops | bytes accessed | tf_op | source)
XLA Modules:
  0.0 154.3 jit_solution(4076238825440869732)
XLA Ops:
  0.6 0.0 copy-start
  0.6 1.3 pad_maximum_fusion
  2.0 22.0 %all_to_all.30.own_ref = bf16[16,4,64,128]{3,2,1,0:T(8,128)(2,1)} all-to-all(bf16[16,4,64,128]{3,2,1,0:T(8,128)(2,1)S(1)} %pad_maximum_fusion), channel_id=1, replica_groups={{0,8,1,9,2,10,3,11,4,12,5,13,6,14,7,15},{16,24,17,25,18,26,19,27,20,28,..., dimensions={0} | all-to-all | bytes 2097152 | tf_op jit(solution)/shard_map/all_to_all | solution.py:302
  24.0 2.2 %totals.1 = f32[16,2,8,128]{3,2,1,0:T(8,128)} custom-call(bf16[16,4,64,128]{3,2,1,0:T(8,128)(2,1)} %all_to_all.30.own_ref), custom_call_target="tpu_custom_call" | custom-call | tf_op jit(solution)/shard_map/totals/pallas_call | solution.py:250
  26.2 20.6 %all_to_all.31.part_ref = f32[16,2,8,128]{3,2,1,0:T(8,128)} all-to-all(f32[16,2,8,128]{3,2,1,0:T(8,128)} %totals.1), channel_id=1, replica_groups={{0,16,32,48,64,80,96,112,128,144,160,176,192,208,224,240},{1,17,33,49,6..., dimensions={0} | all-to-all | bytes 262144 | tf_op jit(solution)/shard_map/all_to_all | solution.py:302
  46.9 1.6 %scan_fwd.1 = f32[16,2,8,128]{3,2,1,0:T(8,128)} custom-call(f32[16,2,8,128]{3,2,1,0:T(8,128)} %all_to_all.31.part_ref), custom_call_target="tpu_custom_call" | custom-call | tf_op jit(solution)/shard_map/scan_fwd/pallas_call | solution.py:262
  48.4 3.5 %all-to-all-start.2 = ((f32[16,2,8,128]{3,2,1,0:T(8,128)}), f32[16,2,8,128]{3,2,1,0:T(8,128)S(1)}, u32[]{:S(2)}, u32[]{:S(2)}) async-start(f32[16,2,8,128]{3,2,1,0:T(8,128)} %scan_fwd.1), calls=%async_computation.2 | async-start | bytes 262144 | tf_op jit(solution)/shard_map/all_to_all | solution.py:302
  52.0 0.0 copy-done
  52.0 0.5 constant_dynamic-slice_fusion.reg_ref
  52.5 9.6 %all-to-all-done.2.before_ref = f32[16,2,8,128]{3,2,1,0:T(8,128)S(1)} async-done(((f32[16,2,8,128]{3,2,1,0:T(8,128)}), f32[16,2,8,128]{3,2,1,0:T(8,128)S(1)}, u32[]{:S(2)}, u32[]{:S(2)}) %all-to-all-start.2) | async-done | bytes 131104 | tf_op jit(solution)/shard_map/all_to_all | solution.py:302
  62.1 0.0 copy-start.1
  62.1 0.7 copy-done.1
  62.7 32.4 %main.1 = (bf16[16,2,64,128]{3,2,1,0:T(8,128)(2,1)}, f32[8,128,128]{2,1,0:T(8,128)}, f32[8,128,128]{2,1,0:T(8,128)}, f32[8,128,128]{2,1,0:T(8,128)}, f32[8,128,128]{2,1,0:T(8,128)}, /*index=5*/f32[16,2,8,128]{3,2,1,0:T(8,128)}) custom-call(bf16[16,4,64,128]{3,2,1,0:T(8,128)(2,1)} %all_to_all.30.own_ref, f32[16,2,8,128]{3,2,1,0:T(8,128)} %copy-done.1, ...), custom_call_target="tpu_custom_call" | custom-call | tf_op jit(solution)/shard_map/main/pallas_call | solution.py:269
  95.1 14.3 %all_to_all.32.part_ref = f32[16,2,8,128]{3,2,1,0:T(8,128)} all-to-all(f32[16,2,8,128]{3,2,1,0:T(8,128)} %get-tuple-element.11), channel_id=1, replica_groups={{0,16,32,48,64,80,96,112,128,144,160,176,192,208,224,240},{1,17,33,49,6..., dimensions={0} | all-to-all | bytes 262144 | tf_op jit(solution)/shard_map/all_to_all | solution.py:302
  109.4 1.6 %scan_rev.1 = f32[16,2,8,128]{3,2,1,0:T(8,128)} custom-call(f32[16,2,8,128]{3,2,1,0:T(8,128)} %all_to_all.32.part_ref), custom_call_target="tpu_custom_call" | custom-call | tf_op jit(solution)/shard_map/scan_rev/pallas_call | solution.py:262
  111.0 14.3 %all_to_all.33.after_ref = f32[16,2,8,128]{3,2,1,0:T(8,128)} all-to-all(f32[16,2,8,128]{3,2,1,0:T(8,128)} %scan_rev.1), channel_id=1, replica_groups={{0,16,32,48,64,80,96,112,128,144,160,176,192,208,224,240},{1,17,33,49,6..., dimensions={0} | all-to-all | bytes 262144 | tf_op jit(solution)/shard_map/all_to_all | solution.py:302
  125.3 0.0 copy-start.2
  125.3 3.4 %final.1 = bf16[16,2,64,128]{3,2,1,0:T(8,128)(2,1)} custom-call(bf16[16,4,64,128]{3,2,1,0:T(8,128)(2,1)} %all_to_all.30.own_ref, f32[16,2,8,128]{3,2,1,0:T(8,128)} %all_to_all.33.after_ref, f32[8,128,128]{2,1,0:T(8,128)} %get-tuple-element.12.dk_ref, f32[8,128,128]{2,1,0:T(8,128)} %get-tuple-element.13.dv_ref, f32[8,128,128]{2,1,0:T(8,128)} %get-tuple-element.14.dgram_ref, ...), custom_call_target="tpu_custom_call" | custom-call | tf_op jit(solution)/shard_map/final/pallas_call | solution.py:288
  128.7 0.0 copy-done.2
  128.7 1.1 pad_maximum_fusion.1
  129.8 23.5 %all_to_all.34 = bf16[16,4,64,128]{3,2,1,0:T(8,128)(2,1)S(1)} all-to-all(bf16[16,4,64,128]{3,2,1,0:T(8,128)(2,1)S(1)} %pad_maximum_fusion.1), channel_id=1, replica_groups={{0,8,1,9,2,10,3,11,4,12,5,13,6,14,7,15},{16,24,17,25,18,26,19,27,20,28,..., dimensions={0} | all-to-all | bytes 2097152 | tf_op jit(solution)/shard_map/all_to_all | solution.py:302
  153.4 1.0 slice_bitcast_fusion
Async XLA Ops:
  0.6 51.3 %copy-start = (f32[2,128]{1,0:T(2,128)S(1)}, f32[2,128]{1,0:T(2,128)}, u32[]{:S(2)}) copy-start(f32[2,128]{1,0:T(2,128)} %param.9) | copy-start | bytes 3076
  48.4 13.7 %all-to-all-start.2 = ((f32[16,2,8,128]{3,2,1,0:T(8,128)}), f32[16,2,8,128]{3,2,1,0:T(8,128)S(1)}, u32[]{:S(2)}, u32[]{:S(2)}) async-start(f32[16,2,8,128]{3,2,1,0:T(8,128)} %scan_fwd.1), calls=%async_computation.2 | async-start | bytes 262144 | tf_op jit(solution)/shard_map/all_to_all | solution.py:302
  62.1 0.7 copy-start.1
  125.3 3.4 %copy-start.2 = (bf16[16,2,64,128]{3,2,1,0:T(8,128)(2,1)S(1)}, bf16[16,2,64,128]{3,2,1,0:T(8,128)(2,1)}, u32[]{:S(2)}) copy-start(bf16[16,2,64,128]{3,2,1,0:T(8,128)(2,1)} %get-tuple-element.10) | copy-start | bytes 1572868

commit v2 on v1

v2 whole, which is shorter than its diff:
```python
import jax
import jax.numpy as jnp
from jax import lax
from jax.experimental import pallas as pl
from jax.experimental.pallas import tpu as pltpu
from jax.sharding import PartitionSpec as P

F32 = jnp.float32
BF16 = jnp.bfloat16
BLOCK = 128
DIM = 128
TILE = 8
PARAMS = pltpu.CompilerParams(vmem_limit_bytes=56 * 1024 * 1024)


def halves(x):
    high = x.astype(BF16)
    return high, (x - high.astype(F32)).astype(BF16)


def thirds(x):
    high = x.astype(BF16)
    rest = x - high.astype(F32)
    mid = rest.astype(BF16)
    return high, mid, (rest - mid.astype(F32)).astype(BF16)


def contract(pairs, left_dim, right_dim):
    left = [a for a, _ in pairs]
    right = [b for _, b in pairs]
    left = left[0] if len(left) == 1 else jnp.concatenate(left, axis=left_dim)
    right = right[0] if len(right) == 1 else jnp.concatenate(right, axis=right_dim)
    return lax.dot_general(
        left, right, (((left_dim,), (right_dim,)), ((), ())), preferred_element_type=F32
    )


def cross(left, right):
    return [(left[0], right[0]), (left[0], right[1]), (left[1], right[0])]


def place_of(chunk, side):
    return 2 * (chunk % 8) + jnp.bitwise_xor(chunk // 8, side)


def owned_rows(ref, block, which, side):
    first = place_of(2 * block, side)
    second = place_of(2 * block + 1, side)
    return jnp.concatenate([ref[first, which], ref[second, which]], axis=0)


def put_rows(ref, block, which, rows, side):
    half = BLOCK // 2
    ref[place_of(2 * block, side), which] = rows[:half]
    ref[place_of(2 * block + 1, side), which] = rows[half:]


def together(steps):
    done = [None] * len(steps)
    live = list(range(len(steps)))
    while live:
        for i in list(live):
            try:
                next(steps[i])
            except StopIteration as end:
                done[i] = end.value
                live.remove(i)
    return done


def factor(mats, count):
    lane = lax.broadcasted_iota(jnp.int32, (TILE, DIM), 1)
    row = lax.broadcasted_iota(jnp.int32, (TILE, DIM), 0)

    def panel(step, start):
        base = pl.multiple_of(step * TILE, TILE)
        rel = lane - base
        inside = (rel >= 0) & (rel < TILE)
        after = rel >= TILE
        unit = jnp.where(rel == row, 1.0, 0.0).astype(F32)
        rows = [mats[n, pl.ds(base, TILE), :] for n in range(count)]
        cols = [
            [jnp.take_along_axis(rows[n], jnp.full((TILE, DIM), 0, jnp.int32) + (base + j), axis=1) for j in range(TILE)]
            for n in range(count)
        ]
        rows = [jnp.where(inside, unit, r) for r in rows]
        for k in range(TILE):
            for n in range(count):
                col = cols[n]
                scale = lax.rsqrt(jnp.broadcast_to(col[k][k : k + 1], (TILE, DIM)))
                pivot = jnp.broadcast_to(rows[n][k : k + 1], (TILE, DIM)) * scale
                mult = jnp.where(row > k, col[k] * scale, 0.0)
                rows[n] = jnp.where(row == k, pivot, rows[n] - mult * pivot)
                for j in range(k + 1, TILE):
                    col[j] = col[j] - mult * jnp.broadcast_to(mult[j : j + 1], (TILE, DIM))
        for n in range(count):
            high, mid, low = thirds(rows[n])
            none = jnp.zeros_like(rows[n])
            lh = jnp.where(after, high.astype(F32), none)
            lm = jnp.where(after, mid.astype(F32), none)
            ll = jnp.where(after, low.astype(F32), none)
            rh, rm, rl = high.astype(F32), mid.astype(F32), low.astype(F32)
            left = jnp.concatenate([lh, lh, lm, lm, lh, ll], axis=0).astype(BF16)
            right = jnp.concatenate([rh, rm, rh, rm, rl, rh], axis=0).astype(BF16)
            left = left[:, start:]
            change = lax.dot_general(
                left, right, (((0,), (0,)), ((), ())), preferred_element_type=F32
            )
            old = mats[n, start:, :]
            keep = jnp.concatenate([inside] * ((DIM - start) // TILE), axis=0)
            mats[n, start:, :] = jnp.where(keep, 0.0, old) - change
            mats[n, pl.ds(base, TILE), :] = rows[n]

    def run(step, carry):
        panel(step, 0)
        return carry

    lax.fori_loop(0, DIM // TILE, run, 0)


def totals_kernel(side_ref, kv_ref, total_ref):
    side = side_ref[0]
    gram = jnp.zeros((DIM, DIM), F32)
    state = jnp.zeros((DIM, DIM), F32)
    for n in range(8):
        k = owned_rows(kv_ref, n, 0, side)
        v = owned_rows(kv_ref, n, 1, side)
        gram = gram + contract([(k, k)], 0, 0)
        state = state + contract([(v, k)], 0, 0)
    total_ref[:DIM] = gram
    total_ref[DIM:] = state


def factor_kernel(side_ref, kv_ref, before_ref, reg_ref, low_ref, inverse, key_inv, mats):
    side = side_ref[0]
    wide = lax.broadcasted_iota(jnp.int32, (DIM, DIM), 1)
    tall = lax.broadcasted_iota(jnp.int32, (DIM, DIM), 0)
    lower = tall >= wide
    gram = before_ref[:DIM] + jnp.where(tall == wide, jnp.broadcast_to(reg_ref[...], (DIM, DIM)), 0.0)
    for n in range(8):
        mats[n] = gram
        if n < 7:
            k = owned_rows(kv_ref, n, 0, side)
            gram = gram + contract([(k, k)], 0, 0)
    factor(mats, 8)

    def middle(n):
        low = halves(jnp.where(lower, mats[n], 0.0))
        yield
        inv = halves(contract(cross(low, low), 0, 0))
        yield
        inverse[n, 0] = inv[0]
        inverse[n, 1] = inv[1]
        k = owned_rows(kv_ref, n, 0, side)
        ki = halves(contract([(k, inv[0]), (k, inv[1])], 1, 0))
        yield
        key_inv[n, 0] = ki[0]
        key_inv[n, 1] = ki[1]
        mats[n] = contract([(ki[0], k), (ki[1], k)], 1, 1) + jnp.where(tall == wide, 1.0, 0.0)

    together([middle(j) for j in range(8)])
    factor(mats, 8)
    for n in range(8):
        low = halves(jnp.where(lower, mats[n], 0.0))
        low_ref[n, 0] = low[0]
        low_ref[n, 1] = low[1]


def solve_kernel(
    side_ref, qg_ref, kv_ref, before_ref, low_ref, inverse, key_inv,
    early_ref, dk_ref, dv_ref, dgram_ref, dstate_ref, total_ref, state_in,
):
    side = side_ref[0]
    wide = lax.broadcasted_iota(jnp.int32, (DIM, DIM), 1)
    tall = lax.broadcasted_iota(jnp.int32, (DIM, DIM), 0)
    lower = tall >= wide
    causal2 = jnp.concatenate([lower, lower], axis=0)
    state = before_ref[DIM:]
    for n in range(8):
        state_in[n] = state
        if n < 7:
            k = owned_rows(kv_ref, n, 0, side)
            v = owned_rows(kv_ref, n, 1, side)
            state = state + contract([(v, k)], 0, 0)

    def solve(n):
        q = owned_rows(qg_ref, n, 0, side)
        g = owned_rows(qg_ref, n, 1, side)
        k = owned_rows(kv_ref, n, 0, side)
        v = owned_rows(kv_ref, n, 1, side)
        st = halves(state_in[n])
        inv = (inverse[n, 0], inverse[n, 1])
        ki = (key_inv[n, 0], key_inv[n, 1])
        low = (low_ref[n, 0], low_ref[n, 1])
        ds = jnp.where(lower, contract([(g, v)], 1, 1), 0.0)
        dsh = halves(ds)
        yield
        du = contract([(g, st[0]), (g, st[1]), (dsh[0], k), (dsh[1], k)], 1, 0)
        duh = halves(du)
        yield
        rhs = (
            jnp.concatenate([q, duh[0]], axis=0),
            jnp.concatenate([jnp.zeros_like(q), duh[1]], axis=0),
        )
        r = halves(contract(cross(rhs, ki), 1, 1))
        yield
        y = halves(jnp.where(causal2, contract(cross(r, low), 1, 1), 0.0))
        yield
        x = halves(-contract(cross(y, low), 1, 0))
        yield
        uz = contract(cross(rhs, inv) + cross(x, ki), 1, 0)
        uzh = halves(uz)
        yield
        ss = jnp.where(causal2, contract([(uzh[0], k), (uzh[1], k)], 1, 1), 0.0)
        u = (uzh[0][:BLOCK], uzh[1][:BLOCK])
        z = (uzh[0][BLOCK:], uzh[1][BLOCK:])
        s = halves(ss[:BLOCK])
        yield
        out = contract(cross(u, st), 1, 1) + contract([(s[0], v), (s[1], v)], 1, 0)
        yield
        put_rows(early_ref, n, 0, out.astype(BF16), side)
        put_rows(early_ref, n, 1, uz[BLOCK:].astype(BF16), side)
        e = halves(ds - ss[BLOCK:])
        yield
        neg = (-s[0], -s[1])
        dk_ref[n] = contract(cross(e, u) + cross(neg, z), 0, 0)
        dv_ref[n] = contract([(s[0], g), (s[1], g)], 0, 0)
        yield
        dstate = contract([(g, u[0]), (g, u[1])], 0, 0)
        yield
        dgram = -contract(cross(z, u), 0, 0)
        dgram_ref[n] = dgram
        dstate_ref[n] = dstate
        return dgram, dstate

    def solve_some(i, carry):
        done = together([solve(8 * i + j) for j in range(8)])
        return (
            carry[0] + sum(a for a, _ in done),
            carry[1] + sum(b for _, b in done),
        )

    zero = jnp.zeros((DIM, DIM), F32)
    sums = lax.fori_loop(0, 1, solve_some, (zero, zero)) if 8 < 8 else solve_some(0, (zero, zero))
    total_ref[:DIM] = sums[0]
    total_ref[DIM:] = sums[1]


def final_kernel(side_ref, kv_ref, after_ref, dk_ref, dv_ref, dgram_ref, dstate_ref, late_ref):
    side = side_ref[0]
    gram = after_ref[:DIM]
    state = after_ref[DIM:]
    later = [None] * 8
    for n in range(7, -1, -1):
        later[n] = (gram, state)
        if n > 0:
            gram = gram + dgram_ref[n]
            state = state + dstate_ref[n]

    def finish(n):
        k = owned_rows(kv_ref, n, 0, side)
        v = owned_rows(kv_ref, n, 1, side)
        sym = halves(later[n][0] + later[n][0].T)
        st = halves(later[n][1])
        yield
        dk = dk_ref[n] + contract([(k, sym[0]), (k, sym[1]), (v, st[0]), (v, st[1])], 1, 0)
        dv = dv_ref[n] + contract([(k, st[0]), (k, st[1])], 1, 1)
        yield
        put_rows(late_ref, n, 0, dk.astype(BF16), side)
        put_rows(late_ref, n, 1, dv.astype(BF16), side)

    together([finish(n) for n in range(8)])


SCALAR = pl.BlockSpec(memory_space=pltpu.SMEM)
VECTOR = pl.BlockSpec(memory_space=pltpu.VMEM)
SQUARE = jax.ShapeDtypeStruct((DIM, DIM), F32)
SQUARES = jax.ShapeDtypeStruct((8, DIM, DIM), F32)
SPLIT = jax.ShapeDtypeStruct((8, 2, DIM, DIM), BF16)
TOKENS = jax.ShapeDtypeStruct((16, 2, BLOCK // 2, DIM), BF16)


def local(kernel, name, outs, count, scratch=()):
    return pl.pallas_call(
        kernel,
        out_shape=outs,
        in_specs=[SCALAR] + [VECTOR] * (count - 1),
        scratch_shapes=list(scratch),
        compiler_params=PARAMS,
        name=name,
    )


AXES = ("seq", "head")


def owner(z, side, head):
    x = head % 2 if side == 0 else 3 - head % 2
    return 32 * z + 8 * x + head // 2


TOKEN_GROUPS = [[owner(z, side, h) for h in range(16)] for z in range(8) for side in range(2)]


def swap(array):
    return lax.all_to_all(array, AXES, 0, 0, axis_index_groups=TOKEN_GROUPS)


def move(array, flip_z, flip_side, keep=None):
    pairs = [
        (owner(z, side, h), owner(z ^ flip_z, side ^ flip_side, h))
        for z in range(8)
        for side in range(2)
        for h in range(16)
        if keep is None or keep(z)
    ]
    return lax.ppermute(array, AXES, pairs)


def carried(part, z, side, reverse):
    def beyond(bit):
        return (bit == 0 if reverse else bit == 1).astype(F32)

    across = move(part, 0, 1)
    along = move(part, 1, 0)
    both = move(part, 1, 1)
    total = (part + across) + (along + both)
    ahead = beyond(side) * across + beyond(z % 2) * (along + both)
    other = move(total, 2, 0)
    ahead = ahead + beyond(z // 2 % 2) * other
    total = total + other
    far = move(total, 7, 0, (lambda z: z >= 4) if reverse else (lambda z: z < 4))
    return ahead + far


def on_device(queries, keys, values, out_grad, regular):
    place = lax.axis_index("seq")
    z = place // 4
    x = place % 4
    side = x // 2
    sides = side.reshape(1).astype(jnp.int32)
    kv = swap(jnp.stack([keys, values], axis=1))
    qg = swap(jnp.stack([queries, out_grad], axis=1))
    reg = lax.dynamic_slice_in_dim(regular, (x % 2) ^ side, 1, 0)
    pair = jax.ShapeDtypeStruct((2 * DIM, DIM), F32)
    gram_before = carried(local(totals_kernel, "totals", pair, 2)(sides, kv), z, side, False)
    state_before = gram_before
    low, inverse, key_inv = local(
        factor_kernel, "factor", (SPLIT, SPLIT, SPLIT), 4, [pltpu.VMEM((8, DIM, DIM), F32)]
    )(sides, kv, gram_before, reg)
    early, dk, dv, dgram, dstate, total = local(
        solve_kernel,
        "solve",
        (TOKENS, SQUARES, SQUARES, SQUARES, SQUARES, jax.ShapeDtypeStruct((2 * DIM, DIM), F32)),
        7,
        [pltpu.VMEM((8, DIM, DIM), F32)],
    )(sides, qg, kv, state_before, low, inverse, key_inv)
    after = carried(total, z, side, True)
    late = local(final_kernel, "final", TOKENS, 7)(sides, kv, after, dk, dv, dgram, dstate)
    early = swap(early)
    late = swap(late)
    return early[:, 0], early[:, 1], late[:, 0], late[:, 1]


def solution(mesh):
    placed = P(None, ("seq", "head"), None)
    return jax.shard_map(
        on_device,
        mesh=mesh,
        in_specs=(placed, placed, placed, placed, P("head", None)),
        out_specs=(placed, placed, placed, placed),
        check_vma=False,
    )
```

time: 155 us -> 131 us (0.85)
  blocking collectives: 94.8 us -> 0 us
  starting transfers between devices: 3.51 us -> 42.6 us
  waiting for transfers between devices: 9.59 us -> 46.3 us
  Pallas kernels: 41.2 us -> 30.6 us
  other arithmetic: 2.46 us -> 6.01 us
  local copies, waits for them, and re-layouts: 2.17 us -> 3.79 us
    all_to_all x5 -> x0, blocking collectives: 94.8 us -> none  [swap(): return lax.all_to_all(array, AXES, 0, 0, axis_index_groups=groups)]
    ppermute x0 -> x10, waiting for transfers between devices: none -> 27.9 us  [move(): return lax.ppermute(array, AXES, pairs)]
    ppermute x0 -> x10, starting transfers between devices: none -> 19.6 us  [move(): return lax.ppermute(array, AXES, pairs)]
    all_to_all x1 -> x4, starting transfers between devices: 3.51 us -> 23 us  [swap(): return lax.all_to_all(array, AXES, 0, 0, axis_index_groups=TOKEN_GROUPS)]
    pallas_call x5 -> x4, Pallas kernels: 41.2 us -> 30.6 us  [the longest x1 18.3 us: on_device(): local(factor_kernel, 'factor', (SPLIT, SPLIT, SPLIT), 4, [pltpu.VMEM((8,...]
    all_to_all x1 -> x4, waiting for transfers between devices: 9.59 us -> 18.4 us  [swap(): return lax.all_to_all(array, AXES, 0, 0, axis_index_groups=TOKEN_GROUPS)]
    add x0 -> x6, other arithmetic: none -> 3.27 us  [the longest x2 1.86 us: carried(): total = part + across + (along + both)]
  transfers between devices with their start and end apart: 1 -> 14, of which waited for: 1 -> 11; matrix products, arithmetic and copies ran while one was open for 0% -> 3% of each run, Pallas kernels for 0% -> 17%
where the time goes in v2:
time: 131 us; the launch traced here: 130 us
  waiting for transfers between devices  46.3 us (35%)
  starting transfers between devices  42.6 us (33%)
  Pallas kernels  30.6 us (23%)
  other arithmetic  6.01 us (5%)
  local copies, waits for them, and re-layouts  3.79 us (3%)
    ppermute x10, waiting for transfers between devices, move(): return lax.ppermute(array, AXES, pairs)  27.9 us
    all_to_all x4, starting transfers between devices, swap(): return lax.all_to_all(array, AXES, 0, 0, axis_index_groups=TOKEN_GROUPS)  23 us
    ppermute x10, starting transfers between devices, move(): return lax.ppermute(array, AXES, pairs)  19.6 us
    all_to_all x4, waiting for transfers between devices, swap(): return lax.all_to_all(array, AXES, 0, 0, axis_index_groups=TOKEN_GROUPS)  18.4 us
    pallas_call x1, Pallas kernels, on_device(): local(factor_kernel, 'factor', (SPLIT, SPLIT, SPLIT), 4, [pltpu.VMEM((8,...  18.3 us
    pallas_call x1, Pallas kernels, on_device(): local(solve_kernel, 'solve', (TOKENS, SQUARES, SQUARES, SQUARES, SQUARES,...  7.04 us
    pallas_call x1, Pallas kernels, on_device(): local(final_kernel, 'final', TOKENS, 7)  3.23 us
  transfers between devices with their start and end apart: 14, of which 11 were waited for; matrix products, arithmetic and copies ran while one was open for 3% of the time, Pallas kernels for 17%

profile of v2, /device:TPU:1, one launch (start us, length us, event | category | flops | bytes accessed | tf_op | source)
XLA Modules:
  0.0 130.2 jit_solution(6770209854931469651)
XLA Ops:
  0.6 1.9 %pad_maximum_fusion.1 = bf16[16,2,64,128]{3,2,1,0:T(8,128)(2,1)} fusion(bf16[16,1,64,128]{3,2,1,0:T(8,128)(2,1)} %bitcast.13, bf16[16,1,64,128]{3,2,1,0:T(8,128)(2,1)} %bitcast.14), kind=kLoop, calls=%fused_computation.1 | loop fusion | flops 262144 | bytes 1048576 | tf_op jit(solution)/shard_map/stack | solution.py:342
  2.5 6.9 %all-to-all-start.1 = ((bf16[16,2,64,128]{3,2,1,0:T(8,128)(2,1)}), bf16[16,2,64,128]{3,2,1,0:T(8,128)(2,1)S(1)}, u32[]{:S(2)}, u32[]{:S(2)}) async-start(bf16[16,2,64,128]{3,2,1,0:T(8,128)(2,1)} %pad_maximum_fusion.1), calls=%async_computation.1 | async-start | bytes 1048576 | tf_op jit(solution)/shard_map/all_to_all | solution.py:306
  9.4 9.6 %all-to-all-done.1.kv_ref = bf16[16,2,64,128]{3,2,1,0:T(8,128)(2,1)S(1)} async-done(((bf16[16,2,64,128]{3,2,1,0:T(8,128)(2,1)}), bf16[16,2,64,128]{3,2,1,0:T(8,128)(2,1)S(1)}, u32[]{:S(2)}, u32[]{:S(2)}) %all-to-all-start.1) | async-done | bytes 524320 | tf_op jit(solution)/shard_map/all_to_all | solution.py:306
  19.9 2.0 %totals.1 = f32[256,128]{1,0:T(8,128)} custom-call(s32[1]{0:T(128)} %bitcast.side_ref, bf16[16,2,64,128]{3,2,1,0:T(8,128)(2,1)} %copy-done.1), custom_call_target="tpu_custom_call" | custom-call | tf_op jit(solution)/shard_map/totals/pallas_call | solution.py:346
  21.9 1.8 %collective-permute-start = (f32[256,128]{1,0:T(8,128)}, f32[256,128]{1,0:T(8,128)S(1)}, u32[]{:S(2)}, u32[]{:S(2)}) collective-permute-start(f32[256,128]{1,0:T(8,128)} %totals.1), channel_id=1, source_target_pairs={{0,24},{8,16},{1,25},{9,17},{2,26},{10,18},{3,27},{11,19},{4,28},{... | collective-permute-start | bytes 393224 | tf_op jit(solution)/shard_map/ppermute | solution.py:317
  23.7 1.6 %collective-permute-start.1 = (f32[256,128]{1,0:T(8,128)}, f32[256,128]{1,0:T(8,128)S(1)}, u32[]{:S(2)}, u32[]{:S(2)}) collective-permute-start(f32[256,128]{1,0:T(8,128)} %totals.1), channel_id=1, source_target_pairs={{0,32},{8,40},{1,33},{9,41},{2,34},{10,42},{3,35},{11,43},{4,36},{... | collective-permute-start | bytes 393224 | tf_op jit(solution)/shard_map/ppermute | solution.py:317
  25.9 2.1 %collective-permute-done = f32[256,128]{1,0:T(8,128)S(1)} collective-permute-done((f32[256,128]{1,0:T(8,128)}, f32[256,128]{1,0:T(8,128)S(1)}, u32[]{:S(2)}, u32[]{:S(2)}) %collective-permute-start) | collective-permute-done | bytes 131104 | tf_op jit(solution)/shard_map/ppermute | solution.py:317
  28.8 3.1 %collective-permute-done.2 = f32[256,128]{1,0:T(8,128)S(1)} collective-permute-done((f32[256,128]{1,0:T(8,128)}, f32[256,128]{1,0:T(8,128)S(1)}, u32[]{:S(2)}, u32[]{:S(2)}) %collective-permute-start.2) | collective-permute-done | bytes 131104 | tf_op jit(solution)/shard_map/ppermute | solution.py:317
  32.8 3.1 %collective-permute-start.3 = (f32[256,128]{1,0:T(8,128)S(1)}, f32[256,128]{1,0:T(8,128)S(1)}, u32[]{:S(2)}, u32[]{:S(2)}) collective-permute-start(f32[256,128]{1,0:T(8,128)S(1)} %add_add_fusion.3), channel_id=1, source_target_pairs={{0,64},{8,72},{1,65},{9,73},{2,66},{10,74},{3,67},{11,75},{4,68},{... | collective-permute-start | bytes 393224 | tf_op jit(solution)/shard_map/ppermute | solution.py:317
  36.7 5.4 %all-to-all-start = ((bf16[16,2,64,128]{3,2,1,0:T(8,128)(2,1)}), bf16[16,2,64,128]{3,2,1,0:T(8,128)(2,1)S(1)}, u32[]{:S(2)}, u32[]{:S(2)}) async-start(bf16[16,2,64,128]{3,2,1,0:T(8,128)(2,1)} %pad_maximum_fusion), calls=%async_computation | async-start | bytes 1048576 | tf_op jit(solution)/shard_map/all_to_all | solution.py:306
  42.1 7.1 %collective-permute-start.4 = (f32[256,128]{1,0:T(8,128)S(1)}, f32[256,128]{1,0:T(8,128)S(1)}, u32[]{:S(2)}, u32[]{:S(2)}) collective-permute-start(f32[256,128]{1,0:T(8,128)S(1)} %add.73), channel_id=1, source_target_pairs={{0,224},{8,232},{1,225},{9,233},{2,226},{10,234},{3,227},{11,235},... | collective-permute-start | bytes 393224 | tf_op jit(solution)/shard_map/ppermute | solution.py:317
  49.9 4.9 %collective-permute-done.4 = f32[256,128]{1,0:T(8,128)S(1)} collective-permute-done((f32[256,128]{1,0:T(8,128)S(1)}, f32[256,128]{1,0:T(8,128)S(1)}, u32[]{:S(2)}, u32[]{:S(2)}) %collective-permute-start.4) | collective-permute-done | bytes 131104 | tf_op jit(solution)/shard_map/ppermute | solution.py:317
  55.5 18.3 %factor.1 = (bf16[8,2,128,128]{3,2,1,0:T(8,128)(2,1)}, bf16[8,2,128,128]{3,2,1,0:T(8,128)(2,1)}, bf16[8,2,128,128]{3,2,1,0:T(8,128)(2,1)}) custom-call(s32[1]{0:T(128)} %bitcast.side_ref, bf16[16,2,64,128]{3,2,1,0:T(8,128)(2,1)} %copy-done.1, f32[256,128]{1,0:T(8,128)} %add_add_fusion.2.before_ref, f32[1,128]{1,0:T(1,128)} %constant_dynamic-slice_fusion.reg_ref), custom_call_target="tpu_custom_call" | custom-call | tf_op jit(solution)/shard_map/factor/pallas_call | solution.py:348
  74.6 7.0 %solve.1 = (bf16[16,2,64,128]{3,2,1,0:T(8,128)(2,1)}, f32[8,128,128]{2,1,0:T(8,128)}, f32[8,128,128]{2,1,0:T(8,128)}, f32[8,128,128]{2,1,0:T(8,128)}, f32[8,128,128]{2,1,0:T(8,128)}, /*index=5*/f32[256,128]{1,0:T(8,128)}) custom-call(s32[1]{0:T(128)} %bitcast.side_ref, bf16[16,2,64,128]{3,2,1,0:T(8,128)(2,1)} %copy-done.2, ...), custom_call_target="tpu_custom_call" | custom-call | tf_op jit(solution)/shard_map/solve/pallas_call | solution.py:351
  81.7 1.8 %collective-permute-start.5 = (f32[256,128]{1,0:T(8,128)}, f32[256,128]{1,0:T(8,128)S(1)}, u32[]{:S(2)}, u32[]{:S(2)}) collective-permute-start(f32[256,128]{1,0:T(8,128)} %get-tuple-element.17), channel_id=1, source_target_pairs={{0,24},{8,16},{1,25},{9,17},{2,26},{10,18},{3,27},{11,19},{4,28},{... | collective-permute-start | bytes 393224 | tf_op jit(solution)/shard_map/ppermute | solution.py:317
  83.5 2.0 %collective-permute-start.7 = (f32[256,128]{1,0:T(8,128)}, f32[256,128]{1,0:T(8,128)S(1)}, u32[]{:S(2)}, u32[]{:S(2)}) collective-permute-start(f32[256,128]{1,0:T(8,128)} %get-tuple-element.17), channel_id=1, source_target_pairs={{0,56},{8,48},{1,57},{9,49},{2,58},{10,50},{3,59},{11,51},{4,60},{... | collective-permute-start | bytes 393224 | tf_op jit(solution)/shard_map/ppermute | solution.py:317
  85.5 2.1 %collective-permute-done.5 = f32[256,128]{1,0:T(8,128)S(1)} collective-permute-done((f32[256,128]{1,0:T(8,128)}, f32[256,128]{1,0:T(8,128)S(1)}, u32[]{:S(2)}, u32[]{:S(2)}) %collective-permute-start.5) | collective-permute-done | bytes 131104 | tf_op jit(solution)/shard_map/ppermute | solution.py:317
  88.0 3.4 %collective-permute-done.7 = f32[256,128]{1,0:T(8,128)S(1)} collective-permute-done((f32[256,128]{1,0:T(8,128)}, f32[256,128]{1,0:T(8,128)S(1)}, u32[]{:S(2)}, u32[]{:S(2)}) %collective-permute-start.7) | collective-permute-done | bytes 131104 | tf_op jit(solution)/shard_map/ppermute | solution.py:317
  92.6 5.8 %all-to-all-start.2 = ((bf16[16,2,64,128]{3,2,1,0:T(8,128)(2,1)}), bf16[16,2,64,128]{3,2,1,0:T(8,128)(2,1)S(1)}, u32[]{:S(2)}, u32[]{:S(2)}) async-start(bf16[16,2,64,128]{3,2,1,0:T(8,128)(2,1)} %get-tuple-element.16), calls=%async_computation.2 | async-start | bytes 1048576 | tf_op jit(solution)/shard_map/all_to_all | solution.py:306
  98.4 1.4 %collective-permute-done.8 = f32[256,128]{1,0:T(8,128)S(1)} collective-permute-done((f32[256,128]{1,0:T(8,128)S(1)}, f32[256,128]{1,0:T(8,128)S(1)}, u32[]{:S(2)}, u32[]{:S(2)}) %collective-permute-start.8) | collective-permute-done | bytes 131104 | tf_op jit(solution)/shard_map/ppermute | solution.py:317
  101.2 9.8 %collective-permute-done.9 = f32[256,128]{1,0:T(8,128)S(1)} collective-permute-done((f32[256,128]{1,0:T(8,128)S(1)}, f32[256,128]{1,0:T(8,128)S(1)}, u32[]{:S(2)}, u32[]{:S(2)}) %collective-permute-start.9) | collective-permute-done | bytes 131104 | tf_op jit(solution)/shard_map/ppermute | solution.py:317
  111.7 3.2 %final.1 = bf16[16,2,64,128]{3,2,1,0:T(8,128)(2,1)} custom-call(s32[1]{0:T(128)} %bitcast.side_ref, bf16[16,2,64,128]{3,2,1,0:T(8,128)(2,1)} %copy-done.1, f32[256,128]{1,0:T(8,128)} %add_add_fusion.after_ref, f32[8,128,128]{2,1,0:T(8,128)} %get-tuple-element.18.dk_ref, f32[8,128,128]{2,1,0:T(8,128)} %get-tuple-element.19.dv_ref, ...), custom_call_target="tpu_custom_call" | custom-call | tf_op jit(solution)/shard_map/final/pallas_call | solution.py:359
  114.9 4.8 %all-to-all-start.3 = ((bf16[16,2,64,128]{3,2,1,0:T(8,128)(2,1)}), bf16[16,2,64,128]{3,2,1,0:T(8,128)(2,1)S(1)}, u32[]{:S(2)}, u32[]{:S(2)}) async-start(bf16[16,2,64,128]{3,2,1,0:T(8,128)(2,1)} %final.1), calls=%async_computation.3 | async-start | bytes 1048576 | tf_op jit(solution)/shard_map/all_to_all | solution.py:306
  120.5 8.8 %all-to-all-done.3 = bf16[16,2,64,128]{3,2,1,0:T(8,128)(2,1)S(1)} async-done(((bf16[16,2,64,128]{3,2,1,0:T(8,128)(2,1)}), bf16[16,2,64,128]{3,2,1,0:T(8,128)(2,1)S(1)}, u32[]{:S(2)}, u32[]{:S(2)}) %all-to-all-start.3) | async-done | bytes 524320 | tf_op jit(solution)/shard_map/all_to_all | solution.py:306
  (29 shorter events, 11.1 us)
Async XLA Ops:
  0.6 48.7 %copy-start = (f32[2,128]{1,0:T(2,128)S(1)}, f32[2,128]{1,0:T(2,128)}, u32[]{:S(2)}) copy-start(f32[2,128]{1,0:T(2,128)} %param.9) | copy-start | bytes 3076
  2.5 16.5 %all-to-all-start.1 = ((bf16[16,2,64,128]{3,2,1,0:T(8,128)(2,1)}), bf16[16,2,64,128]{3,2,1,0:T(8,128)(2,1)S(1)}, u32[]{:S(2)}, u32[]{:S(2)}) async-start(bf16[16,2,64,128]{3,2,1,0:T(8,128)(2,1)} %pad_maximum_fusion.1), calls=%async_computation.1 | async-start | bytes 1048576 | tf_op jit(solution)/shard_map/all_to_all | solution.py:306
  19.1 0.8 copy-start.1
  21.9 14.0 %copy-start.3 = (bf16[16,64,128]{2,1,0:T(8,128)(2,1)S(1)}, bf16[16,64,128]{2,1,0:T(8,128)(2,1)}, u32[]{:S(2)}) copy-start(bf16[16,64,128]{2,1,0:T(8,128)(2,1)} %param.8) | copy-start | bytes 786436
  21.9 14.0 %copy-start.4 = (bf16[16,64,128]{2,1,0:T(8,128)(2,1)S(1)}, bf16[16,64,128]{2,1,0:T(8,128)(2,1)}, u32[]{:S(2)}) copy-start(bf16[16,64,128]{2,1,0:T(8,128)(2,1)} %param.5) | copy-start | bytes 786436
  21.9 6.1 %collective-permute-start = (f32[256,128]{1,0:T(8,128)}, f32[256,128]{1,0:T(8,128)S(1)}, u32[]{:S(2)}, u32[]{:S(2)}) collective-permute-start(f32[256,128]{1,0:T(8,128)} %totals.1), channel_id=1, source_target_pairs={{0,24},{8,16},{1,25},{9,17},{2,26},{10,18},{3,27},{11,19},{4,28},{... | collective-permute-start | bytes 393224 | tf_op jit(solution)/shard_map/ppermute | solution.py:317
  23.7 5.1 %collective-permute-start.1 = (f32[256,128]{1,0:T(8,128)}, f32[256,128]{1,0:T(8,128)S(1)}, u32[]{:S(2)}, u32[]{:S(2)}) collective-permute-start(f32[256,128]{1,0:T(8,128)} %totals.1), channel_id=1, source_target_pairs={{0,32},{8,40},{1,33},{9,41},{2,34},{10,42},{3,35},{11,43},{4,36},{... | collective-permute-start | bytes 393224 | tf_op jit(solution)/shard_map/ppermute | solution.py:317
  25.3 6.5 %collective-permute-start.2 = (f32[256,128]{1,0:T(8,128)}, f32[256,128]{1,0:T(8,128)S(1)}, u32[]{:S(2)}, u32[]{:S(2)}) collective-permute-start(f32[256,128]{1,0:T(8,128)} %totals.1), channel_id=1, source_target_pairs={{0,56},{8,48},{1,57},{9,49},{2,58},{10,50},{3,59},{11,51},{4,60},{... | collective-permute-start | bytes 393224 | tf_op jit(solution)/shard_map/ppermute | solution.py:317
  32.8 9.3 %collective-permute-start.3 = (f32[256,128]{1,0:T(8,128)S(1)}, f32[256,128]{1,0:T(8,128)S(1)}, u32[]{:S(2)}, u32[]{:S(2)}) collective-permute-start(f32[256,128]{1,0:T(8,128)S(1)} %add_add_fusion.3), channel_id=1, source_target_pairs={{0,64},{8,72},{1,65},{9,73},{2,66},{10,74},{3,67},{11,75},{4,68},{... | collective-permute-start | bytes 393224 | tf_op jit(solution)/shard_map/ppermute | solution.py:317
  36.7 37.1 %all-to-all-start = ((bf16[16,2,64,128]{3,2,1,0:T(8,128)(2,1)}), bf16[16,2,64,128]{3,2,1,0:T(8,128)(2,1)S(1)}, u32[]{:S(2)}, u32[]{:S(2)}) async-start(bf16[16,2,64,128]{3,2,1,0:T(8,128)(2,1)} %pad_maximum_fusion), calls=%async_computation | async-start | bytes 1048576 | tf_op jit(solution)/shard_map/all_to_all | solution.py:306
  42.1 12.7 %collective-permute-start.4 = (f32[256,128]{1,0:T(8,128)S(1)}, f32[256,128]{1,0:T(8,128)S(1)}, u32[]{:S(2)}, u32[]{:S(2)}) collective-permute-start(f32[256,128]{1,0:T(8,128)S(1)} %add.73), channel_id=1, source_target_pairs={{0,224},{8,232},{1,225},{9,233},{2,226},{10,234},{3,227},{11,235},... | collective-permute-start | bytes 393224 | tf_op jit(solution)/shard_map/ppermute | solution.py:317
  73.8 0.8 copy-start.2
  81.7 6.0 %collective-permute-start.5 = (f32[256,128]{1,0:T(8,128)}, f32[256,128]{1,0:T(8,128)S(1)}, u32[]{:S(2)}, u32[]{:S(2)}) collective-permute-start(f32[256,128]{1,0:T(8,128)} %get-tuple-element.17), channel_id=1, source_target_pairs={{0,24},{8,16},{1,25},{9,17},{2,26},{10,18},{3,27},{11,19},{4,28},{... | collective-permute-start | bytes 393224 | tf_op jit(solution)/shard_map/ppermute | solution.py:317
  83.5 4.5 %collective-permute-start.6 = (f32[256,128]{1,0:T(8,128)}, f32[256,128]{1,0:T(8,128)S(1)}, u32[]{:S(2)}, u32[]{:S(2)}) collective-permute-start(f32[256,128]{1,0:T(8,128)} %get-tuple-element.17), channel_id=1, source_target_pairs={{0,32},{8,40},{1,33},{9,41},{2,34},{10,42},{3,35},{11,43},{4,36},{... | collective-permute-start | bytes 393224 | tf_op jit(solution)/shard_map/ppermute | solution.py:317
  83.5 7.9 %collective-permute-start.7 = (f32[256,128]{1,0:T(8,128)}, f32[256,128]{1,0:T(8,128)S(1)}, u32[]{:S(2)}, u32[]{:S(2)}) collective-permute-start(f32[256,128]{1,0:T(8,128)} %get-tuple-element.17), channel_id=1, source_target_pairs={{0,56},{8,48},{1,57},{9,49},{2,58},{10,50},{3,59},{11,51},{4,60},{... | collective-permute-start | bytes 393224 | tf_op jit(solution)/shard_map/ppermute | solution.py:317
  92.3 7.5 %collective-permute-start.8 = (f32[256,128]{1,0:T(8,128)S(1)}, f32[256,128]{1,0:T(8,128)S(1)}, u32[]{:S(2)}, u32[]{:S(2)}) collective-permute-start(f32[256,128]{1,0:T(8,128)S(1)} %add_add_fusion.1), channel_id=1, source_target_pairs={{0,64},{8,72},{1,65},{9,73},{2,66},{10,74},{3,67},{11,75},{4,68},{... | collective-permute-start | bytes 393224 | tf_op jit(solution)/shard_map/ppermute | solution.py:317
  92.6 22.3 %all-to-all-start.2 = ((bf16[16,2,64,128]{3,2,1,0:T(8,128)(2,1)}), bf16[16,2,64,128]{3,2,1,0:T(8,128)(2,1)S(1)}, u32[]{:S(2)}, u32[]{:S(2)}) async-start(bf16[16,2,64,128]{3,2,1,0:T(8,128)(2,1)} %get-tuple-element.16), calls=%async_computation.2 | async-start | bytes 1048576 | tf_op jit(solution)/shard_map/all_to_all | solution.py:306
  99.8 11.1 %collective-permute-start.9 = (f32[256,128]{1,0:T(8,128)S(1)}, f32[256,128]{1,0:T(8,128)S(1)}, u32[]{:S(2)}, u32[]{:S(2)}) collective-permute-start(f32[256,128]{1,0:T(8,128)S(1)} %add.82), channel_id=1, source_target_pairs={{128,96},{136,104},{129,97},{137,105},{130,98},{138,106},{131,99},... | collective-permute-start | bytes 393224 | tf_op jit(solution)/shard_map/ppermute | solution.py:317
  114.9 14.5 %all-to-all-start.3 = ((bf16[16,2,64,128]{3,2,1,0:T(8,128)(2,1)}), bf16[16,2,64,128]{3,2,1,0:T(8,128)(2,1)S(1)}, u32[]{:S(2)}, u32[]{:S(2)}) async-start(bf16[16,2,64,128]{3,2,1,0:T(8,128)(2,1)} %final.1), calls=%async_computation.3 | async-start | bytes 1048576 | tf_op jit(solution)/shard_map/all_to_all | solution.py:306
